TPU v7x, 256 devices: a whole 4x4x8 slice. The times are simulated.
256 devices in a mesh: row: 16 (over y, x), col: 16 (over z, core).
Axes of the slice: x: 4, y: 4, z: 8, core: 2. Of those that a mesh axis runs over, the one named last changes fastest.
Arguments:
- hidden_in: bfloat16 [1024, 4096], P('col', 'row'), may hold values from -250 to 250
- norm_gain: bfloat16 [4096], P('row'), may hold values from 0.099609375 to 1.8984375
- w_qkv: bfloat16 [4096, 6144], P('row', 'col'), may hold values from -0.125 to 0.125
- w_out: bfloat16 [4096, 4096], P('row', 'col'), may hold values from -0.125 to 0.125
- cache_k: bfloat16 [16, 4096, 1024], P('col', 'row'), may hold values from -1300 to 1300
- value_cache: bfloat16 [16, 4096, 1024], P('col', 'row'), may hold values from -6 to 6
- cache_len: int32 [16], P('col'), may hold values from 1 to 4096, as said below
- parents: int32 [16, 64], P('col'), may hold values from -1 to 62, as said below
Outputs:
- update: bfloat16 [1024, 4096], P('col', 'row')
Inputs may be any that keep to these rules, and one draw needn't show every extreme that they name: Slots 0 to cache_len - 1 of a request's window are filled; some request fills all 4096 slots. `parents`: slot 0 of every request is the root with parent -1; every other slot's parent is an earlier slot of the same request; slot 63 has parent 64 - 2.
All inputs are finite; a program needn't handle non-finite values.
Results may differ from a plain program's by a relative error of at most 0.011.
The roundings to bfloat16 on the way count: a program that leaves them out, or rounds other values in their place, can miss the bound.
Values may be sent and summed in bfloat16 or wider, within the bound.
A program may use at most 128 MiB of HBM per device.

v0:
```python
import jax
import jax.numpy as jnp
from jax import lax
from jax.sharding import PartitionSpec as P

D = 4096
QUERY_HEADS = 32
KEY_VALUE_HEADS = 8
HEAD_SIZE = 128
masked_score = -1e30


def ancestors(parents):
    draft_tree = parents.shape[1]
    slot_ids = jnp.arange(draft_tree, dtype=jnp.int32)
    parent_links = (parents[:, :, None] == slot_ids[None, None, :]).astype(jnp.float32)
    reachable = parent_links + jnp.eye(draft_tree, dtype=jnp.float32)[None]
    for squaring in range(max(1, (draft_tree - 1).bit_length())):
        product = jnp.einsum("rij,rjk->rik", reachable, reachable, precision=lax.Precision.HIGHEST)
        reachable = (product > 0.5).astype(jnp.float32)
    return reachable > 0.5


def row_reduce(partial, axis_name, sent=jnp.float32):
    count = lax.axis_size(axis_name)
    rows, cols = partial.shape
    pieces = partial.reshape(rows, count, cols // count).transpose(1, 0, 2).astype(sent)
    received = lax.all_to_all(pieces, axis_name, 0, 0)
    return jnp.sum(received.astype(jnp.float32), axis=0)


def row_gather(value, axis_name):
    count = lax.axis_size(axis_name)
    copies = jnp.broadcast_to(value[None], (count,) + value.shape)
    return lax.all_to_all(copies, axis_name, 0, 0)


def shards(hidden_in, norm_gain, w_qkv, w_out, cache_k, value_cache, cache_len, parents):
    rows_here = hidden_in.shape[0]
    request_list = cache_k.shape[0]
    token_positions = cache_k.shape[1]
    draft_tree = parents.shape[1]
    head_groups = QUERY_HEADS // KEY_VALUE_HEADS
    row_count = lax.axis_size("row")
    heads_dev = QUERY_HEADS // row_count
    row_index = lax.axis_index("row")
    score_scale = HEAD_SIZE ** (-0.5)
    features = hidden_in.astype(jnp.float32)
    squares = jnp.sum(row_gather(jnp.sum(features * features, axis=1), "row"), axis=0)
    row_scale = lax.rsqrt(squares / D + 1e-05)
    normed = (features * row_scale[:, None] * norm_gain.astype(jnp.float32)[None, :]).astype(
        jnp.bfloat16
    )
    half = w_qkv.shape[1] // 2
    halves = []
    for part in (w_qkv[:, :half], w_qkv[:, half:]):
        partial_value = jnp.dot(
            normed,
            lax.all_gather(part, "col", axis=1, tiled=True),
            preferred_element_type=jnp.float32,
        )
        halves.append(row_reduce(partial_value, "row"))
    summed = jnp.concatenate(halves, axis=1).astype(jnp.bfloat16)
    projected_output = row_gather(summed, "row").transpose(1, 0, 2).reshape(rows_here, -1)
    query_block = projected_output[:, : QUERY_HEADS * HEAD_SIZE].reshape(
        request_list, draft_tree, KEY_VALUE_HEADS, head_groups, HEAD_SIZE
    )
    new_key_block = projected_output[
        :, QUERY_HEADS * HEAD_SIZE : (QUERY_HEADS + KEY_VALUE_HEADS) * HEAD_SIZE
    ].reshape(request_list, draft_tree, KEY_VALUE_HEADS, HEAD_SIZE)
    new_value_block = projected_output[:, (QUERY_HEADS + KEY_VALUE_HEADS) * HEAD_SIZE :].reshape(
        request_list, draft_tree, KEY_VALUE_HEADS, HEAD_SIZE
    )
    first_slot = row_index * token_positions
    slot_ids = first_slot + jnp.arange(token_positions, dtype=jnp.int32)

    def cache_part(request_item):
        query_rows, cached_key_rows, cached_value_rows, length = request_item
        key_row_block = cached_key_rows.reshape(token_positions, KEY_VALUE_HEADS, HEAD_SIZE)
        value_row_block = cached_value_rows.reshape(token_positions, KEY_VALUE_HEADS, HEAD_SIZE)
        scores = (
            jnp.einsum(
                "tkgd,pkd->kgtp", query_rows, key_row_block, preferred_element_type=jnp.float32
            )
            * score_scale
        )
        visible = (slot_ids < length)[None, None, None, :]
        scores = jnp.where(visible, scores, masked_score)
        highest = jnp.max(scores, axis=-1)
        weights = jnp.where(visible, jnp.exp(scores - highest[..., None]), 0.0)
        totals = jnp.sum(weights, axis=-1)
        blended = jnp.einsum(
            "kgtp,pkd->kgtd",
            weights.astype(jnp.bfloat16),
            value_row_block,
            preferred_element_type=jnp.float32,
        )
        stats = jnp.concatenate(
            [highest.reshape(QUERY_HEADS, draft_tree), totals.reshape(QUERY_HEADS, draft_tree)],
            axis=-1,
        )
        return jnp.concatenate(
            [blended.reshape(QUERY_HEADS, draft_tree, HEAD_SIZE), stats[:, None, :]], axis=1
        )

    packed = lax.map(cache_part, (query_block, cache_k, value_cache, cache_len))
    packed = packed.reshape(request_list, row_count, heads_dev, draft_tree + 1, HEAD_SIZE)
    gathered = lax.all_to_all(packed, "row", 1, 1)
    block_blend = gathered[:, :, :, :draft_tree, :]
    block_max = gathered[:, :, :, draft_tree, :draft_tree]
    block_total = gathered[:, :, :, draft_tree, draft_tree : 2 * draft_tree]
    allowed = ancestors(parents)[:, None, :, :]
    query_heads = projected_output[:, : QUERY_HEADS * HEAD_SIZE].reshape(
        request_list, draft_tree, QUERY_HEADS, HEAD_SIZE
    )
    query_own = lax.dynamic_slice_in_dim(query_heads, row_index * heads_dev, heads_dev, 2)
    key_own = lax.dynamic_slice_in_dim(
        jnp.repeat(new_key_block, head_groups, axis=2), row_index * heads_dev, heads_dev, 2
    )
    value_own = lax.dynamic_slice_in_dim(
        jnp.repeat(new_value_block, head_groups, axis=2), row_index * heads_dev, heads_dev, 2
    )
    tree_scores = (
        jnp.einsum("rthd,rshd->rhts", query_own, key_own, preferred_element_type=jnp.float32)
        * score_scale
    )
    tree_scores = jnp.where(allowed, tree_scores, masked_score)
    tree_max = jnp.max(tree_scores, axis=-1)
    tree_weights = jnp.where(allowed, jnp.exp(tree_scores - tree_max[..., None]), 0.0)
    tree_total = jnp.sum(tree_weights, axis=-1)
    tree_blend = jnp.einsum(
        "rhts,rshd->rhtd",
        tree_weights.astype(jnp.bfloat16),
        value_own,
        preferred_element_type=jnp.float32,
    )
    joint_max = jnp.maximum(jnp.max(block_max, axis=1), tree_max)
    block_scale = jnp.exp(block_max - joint_max[:, None])
    tree_scale = jnp.exp(tree_max - joint_max)
    numerator = (
        jnp.sum(block_blend * block_scale[..., None], axis=1) + tree_blend * tree_scale[..., None]
    )
    denominator = jnp.sum(block_total * block_scale, axis=1) + tree_total * tree_scale
    attended = (numerator / denominator[..., None]).astype(jnp.bfloat16)
    attended = attended.transpose(0, 2, 1, 3).reshape(rows_here, heads_dev * HEAD_SIZE)
    partial_out = jnp.dot(
        attended,
        lax.all_gather(w_out, "col", axis=1, tiled=True),
        preferred_element_type=jnp.float32,
    )
    return row_reduce(partial_out, "row", jnp.bfloat16).astype(jnp.bfloat16)


def solution(mesh):
    placed = (
        P("col", "row"),
        P("row"),
        P("row", "col"),
        P("row", "col"),
        P("col", "row", None),
        P("col", "row", None),
        P("col"),
        P("col", None),
    )
    return jax.shard_map(
        shards, mesh=mesh, in_specs=placed, out_specs=P("col", "row"), check_vma=False
    )
```

profile of v0, /device:TPU:1, one launch (start us, length us, event | category | flops | bytes accessed | tf_op | source)
XLA Modules:
  0.0 190.4 jit_solution(11534638111007706878)
XLA Ops:
  6.5 1.1 fusion.53
  10.7 7.6 %all-to-all-start = ((f32[16,1,64]{2,1,0:T(1,128)}), f32[16,1,64]{2,1,0:T(1,128)S(1)}, u32[]{:S(2)}, u32[]{:S(2)}) async-start(f32[16,1,64]{2,1,0:T(1,128)} %broadcast_in_dim.88), calls=%async_computation | async-start | bytes 16384 | tf_op jit(solution)/shard_map/all_to_all | solution.py:35
  19.7 5.0 %all-to-all-done = f32[16,1,64]{2,1,0:T(1,128)S(1)} async-done(((f32[16,1,64]{2,1,0:T(1,128)}), f32[16,1,64]{2,1,0:T(1,128)S(1)}, u32[]{:S(2)}, u32[]{:S(2)}) %all-to-all-start) | async-done | bytes 4128 | tf_op jit(solution)/shard_map/all_to_all | solution.py:35
  24.7 27.6 %all-gather.6.cloned.1.call-done = bf16[256,3072]{0,1:T(8,128)(2,1)} async-done(((bf16[256,192]{0,1:T(8,128)(2,1)}), bf16[256,3072]{0,1:T(8,128)(2,1)}) %all-gather.6.cloned.1.call-update) | async-done | bytes 1572880 | tf_op jit(solution)/shard_map/all_gather | solution.py:59
  52.3 2.0 %fusion.43 = f32[64,3072]{1,0:T(8,128)S(1)} fusion(bf16[256,3072]{0,1:T(8,128)(2,1)} %all-gather.6.cloned.1.call-done, bf16[64,256]{1,0:T(8,128)(2,1)} %param.8, f32[256]{0:T(256)S(1)} %convert_element_type.93, f32[64]{0:T(128)S(1)} %add_rsqrt_fusion), kind=kOutput, calls=%fused_computation.71 | convolution fusion | flops 100728832 | bytes 2393344 | tf_op jit(solution)/shard_map/dot_general | solution.py:57
  54.8 1.6 copy.141
  56.4 6.6 %all-to-all-start.2 = ((f32[16,64,192]{2,1,0:T(8,128)}), f32[16,64,192]{2,1,0:T(8,128)S(1)}, u32[]{:S(2)}, u32[]{:S(2)}) async-start(f32[16,64,192]{2,1,0:T(8,128)} %bitcast.99), calls=%async_computation.2 | async-start | bytes 2097152 | tf_op jit(solution)/shard_map/all_to_all | solution.py:28
  63.0 28.7 %all-gather.4.cloned.1.call-done = bf16[256,3072]{0,1:T(8,128)(2,1)} async-done(((bf16[256,192]{0,1:T(8,128)(2,1)}), bf16[256,3072]{0,1:T(8,128)(2,1)}) %all-gather.4.cloned.1.call-update) | async-done | bytes 1572880 | tf_op jit(solution)/shard_map/all_gather | solution.py:59
  91.7 2.0 %fusion.45 = f32[64,3072]{1,0:T(8,128)S(1)} fusion(bf16[256,3072]{0,1:T(8,128)(2,1)} %all-gather.4.cloned.1.call-done, bf16[64,256]{1,0:T(8,128)(2,1)S(1)} %copy-done.4, f32[256]{0:T(256)S(1)} %convert_element_type.93, f32[64]{0:T(128)S(1)} %add_rsqrt_fusion), kind=kOutput, calls=%fused_computation.72 | convolution fusion | flops 100728832 | bytes 2393344 | tf_op jit(solution)/shard_map/dot_general | solution.py:57
  94.2 1.6 copy.142
  95.8 6.7 %all-to-all-start.1 = ((f32[16,64,192]{2,1,0:T(8,128)}), f32[16,64,192]{2,1,0:T(8,128)S(1)}, u32[]{:S(2)}, u32[]{:S(2)}) async-start(f32[16,64,192]{2,1,0:T(8,128)} %bitcast.100), calls=%async_computation.1 | async-start | bytes 2097152 | tf_op jit(solution)/shard_map/all_to_all | solution.py:28
  104.4 14.5 %all-to-all-done.1 = f32[16,64,192]{2,1,0:T(8,128)S(1)} async-done(((f32[16,64,192]{2,1,0:T(8,128)}), f32[16,64,192]{2,1,0:T(8,128)S(1)}, u32[]{:S(2)}, u32[]{:S(2)}) %all-to-all-start.1) | async-done | bytes 786464 | tf_op jit(solution)/shard_map/all_to_all | solution.py:28
  119.1 1.0 broadcast_in_dim.89
  120.1 4.5 %all-to-all-start.3 = ((bf16[16,64,384]{2,1,0:T(8,128)(2,1)}), bf16[16,64,384]{2,1,0:T(8,128)(2,1)S(1)}, u32[]{:S(2)}, u32[]{:S(2)}) async-start(bf16[16,64,384]{2,1,0:T(8,128)(2,1)} %broadcast_in_dim.89), calls=%async_computation.3 | async-start | bytes 1572864 | tf_op jit(solution)/shard_map/all_to_all | solution.py:35
  125.3 12.4 %all-to-all-done.3 = bf16[16,64,384]{2,1,0:T(8,128)(2,1)S(1)} async-done(((bf16[16,64,384]{2,1,0:T(8,128)(2,1)}), bf16[16,64,384]{2,1,0:T(8,128)(2,1)S(1)}, u32[]{:S(2)}, u32[]{:S(2)}) %all-to-all-start.3) | async-done | bytes 786464 | tf_op jit(solution)/shard_map/all_to_all | solution.py:35
  143.1 1.5 maximum_maximum_fusion
  144.6 3.9 %all-to-all-start.4 = ((f32[1,16,2,65,128]{4,2,3,0,1:T(2,128)}), f32[1,16,2,65,128]{4,2,3,0,1:T(2,128)S(1)}, u32[]{:S(2)}, u32[]{:S(2)}) async-start(f32[1,16,2,65,128]{4,2,3,0,1:T(2,128)} %maximum_maximum_fusion), calls=%async_computation.4 | async-start | bytes 2129920 | tf_op jit(solution)/shard_map/all_to_all | solution.py:108
  148.8 3.3 %copy.103 = bf16[4096,256]{1,0:T(8,128)(2,1)S(1)} copy(bf16[4096,256]{0,1:T(8,128)(2,1)} %bitcast.106) | data formatting | bytes 4194304 | tf_op jit(solution)/shard_map/dot_general | solution.py:146
  152.0 1.1 copy.119
  153.2 1.0 slice_bitcast_fusion
  154.6 9.1 %all-to-all-done.4 = f32[1,16,2,65,128]{4,2,3,0,1:T(2,128)S(1)} async-done(((f32[1,16,2,65,128]{4,2,3,0,1:T(2,128)}), f32[1,16,2,65,128]{4,2,3,0,1:T(2,128)S(1)}, u32[]{:S(2)}, u32[]{:S(2)}) %all-to-all-start.4) | async-done | bytes 1064992 | tf_op jit(solution)/shard_map/all_to_all | solution.py:108
  163.8 1.0 copy.98
  164.9 2.2 %fusion.14 = f32[2,64,128]{2,0,1:T(2,128)S(1)} fusion(f32[1,16,2,65,128]{4,2,3,0,1:T(2,128)S(1)} %all-to-all-done.4, f32[16,2,64]{1,2,0:T(8,128)} %copy.98), kind=kLoop, calls=%fused_computation.27 | loop fusion | flops 507904 | bytes 1122304 | tf_op jit(solution)/shard_map/reduce_sum | solution.py:141
  168.4 14.8 %all_to_all.31 = bf16[16,64,256]{2,1,0:T(8,128)(2,1)S(1)} all-to-all(bf16[16,64,256]{2,1,0:T(8,128)(2,1)S(1)} %fusion.4), channel_id=1, replica_groups=mesh['row'=16,'col'=16] {'row'}, dimensions={0} | all-to-all | bytes 1048576 | tf_op jit(solution)/shard_map/all_to_all | solution.py:28
  (66 shorter events, 15.5 us)
Async XLA Ops:
  6.5 45.7 %all-gather.6.cloned.1.call-start = ((), (), s32[]{:S(2)}) async-start(), calls=%async_computation.7 | async-start | bytes 1671168 | tf_op jit(solution)/shard_map/all_gather | solution.py:59
  8.4 83.3 %all-gather.4.cloned.1.call-start = ((), (), s32[]{:S(2)}) async-start(), calls=%async_computation.6 | async-start | bytes 1671168 | tf_op jit(solution)/shard_map/all_gather | solution.py:59
  10.7 13.9 %all-to-all-start = ((f32[16,1,64]{2,1,0:T(1,128)}), f32[16,1,64]{2,1,0:T(1,128)S(1)}, u32[]{:S(2)}, u32[]{:S(2)}) async-start(f32[16,1,64]{2,1,0:T(1,128)} %broadcast_in_dim.88), calls=%async_computation | async-start | bytes 16384 | tf_op jit(solution)/shard_map/all_to_all | solution.py:35
  18.3 130.5 %all-gather.8.cloned.1.call-start = ((), (), s32[]{:S(2)}) async-start(), calls=%async_computation.8 | async-start | bytes 2228224 | tf_op jit(solution)/shard_map/all_gather | solution.py:148
  54.8 36.9 %copy-start.4 = (bf16[64,256]{1,0:T(8,128)(2,1)S(1)}, bf16[64,256]{1,0:T(8,128)(2,1)}, u32[]{:S(2)}) copy-start(bf16[64,256]{1,0:T(8,128)(2,1)} %param.8) | copy-start | bytes 98308
  56.4 39.5 %all-to-all-start.2 = ((f32[16,64,192]{2,1,0:T(8,128)}), f32[16,64,192]{2,1,0:T(8,128)S(1)}, u32[]{:S(2)}, u32[]{:S(2)}) async-start(f32[16,64,192]{2,1,0:T(8,128)} %bitcast.99), calls=%async_computation.2 | async-start | bytes 2097152 | tf_op jit(solution)/shard_map/all_to_all | solution.py:28
  94.2 8.9 %copy-start.1 = (bf16[1,256,1024]{2,1,0:T(8,128)(2,1)S(1)}, bf16[1,256,1024]{2,1,0:T(8,128)(2,1)}, u32[]{:S(2)}) copy-start(bf16[1,256,1024]{2,1,0:T(8,128)(2,1)} %param.12) | copy-start | bytes 1572868
  95.8 8.2 %copy-start.2 = (bf16[1,256,1024]{2,1,0:T(8,128)(2,1)S(1)}, bf16[1,256,1024]{2,1,0:T(8,128)(2,1)}, u32[]{:S(2)}) copy-start(bf16[1,256,1024]{2,1,0:T(8,128)(2,1)} %param.13) | copy-start | bytes 1572868
  95.8 8.3 %copy-start.5 = (s32[1,64]{1,0:T(1,128)S(1)}, s32[1,64]{1,0:T(1,128)}, u32[]{:S(2)}) copy-start(s32[1,64]{1,0:T(1,128)} %param.15) | copy-start | bytes 772
  95.8 23.1 %all-to-all-start.1 = ((f32[16,64,192]{2,1,0:T(8,128)}), f32[16,64,192]{2,1,0:T(8,128)S(1)}, u32[]{:S(2)}, u32[]{:S(2)}) async-start(f32[16,64,192]{2,1,0:T(8,128)} %bitcast.100), calls=%async_computation.1 | async-start | bytes 2097152 | tf_op jit(solution)/shard_map/all_to_all | solution.py:28
  120.1 17.6 %all-to-all-start.3 = ((bf16[16,64,384]{2,1,0:T(8,128)(2,1)}), bf16[16,64,384]{2,1,0:T(8,128)(2,1)S(1)}, u32[]{:S(2)}, u32[]{:S(2)}) async-start(bf16[16,64,384]{2,1,0:T(8,128)(2,1)} %broadcast_in_dim.89), calls=%async_computation.3 | async-start | bytes 1572864 | tf_op jit(solution)/shard_map/all_to_all | solution.py:35
  137.7 2.3 %copy-start.3 = (bf16[32,8,8,128]{3,2,1,0:T(8,128)(2,1)S(1)}, bf16[32,8,8,128]{3,2,1,0:T(8,128)(2,1)}, u32[]{:S(2)}) copy-start(bf16[32,8,8,128]{3,2,1,0:T(8,128)(2,1)} %copy.117) | copy-start | bytes 1572868
  137.8 0.9 copy-start
  144.6 19.2 %all-to-all-start.4 = ((f32[1,16,2,65,128]{4,2,3,0,1:T(2,128)}), f32[1,16,2,65,128]{4,2,3,0,1:T(2,128)S(1)}, u32[]{:S(2)}, u32[]{:S(2)}) async-start(f32[1,16,2,65,128]{4,2,3,0,1:T(2,128)} %maximum_maximum_fusion), calls=%async_computation.4 | async-start | bytes 2129920 | tf_op jit(solution)/shard_map/all_to_all | solution.py:108
Sparse Core Ops, SparseCore 0:
  9.2 43.0 all-gather.5
  54.1 37.5 all-gather.3
  93.5 39.2 all-gather.7
where the time goes:
time: 191 us; the launch traced here: 190 us
  waiting for transfers between devices  98 us (51%)
  starting transfers between devices  29.4 us (15%)
  local copies, waits for them, and re-layouts  19.3 us (10%)
  blocking collectives  14.8 us (8%)
  between operations  14.1 us (7%)
  other arithmetic  7.51 us (4%)
  matrix products  7.26 us (4%)
    all_gather x2, waiting for transfers between devices, shards(): lax.all_gather(part, 'col', axis=1, tiled=True)  56.3 us
    all_to_all x2, waiting for transfers between devices, row_gather(): return lax.all_to_all(copies, axis_name, 0, 0)  17.4 us
    all_to_all x1, blocking collectives, row_reduce(): received = lax.all_to_all(pieces, axis_name, 0, 0)  14.8 us
    all_to_all x2, waiting for transfers between devices, row_reduce(): received = lax.all_to_all(pieces, axis_name, 0, 0)  14.5 us
    all_to_all x2, starting transfers between devices, row_reduce(): received = lax.all_to_all(pieces, axis_name, 0, 0)  13.3 us
    all_to_all x2, starting transfers between devices, row_gather(): return lax.all_to_all(copies, axis_name, 0, 0)  12.1 us
    all_to_all x1, waiting for transfers between devices, shards(): gathered = lax.all_to_all(packed, 'row', 1, 1)  9.12 us
    unnamed x19, local copies, waits for them, and re-layouts  6.45 us
  transfers between devices with their start and end apart: 8, of which 6 were waited for; matrix products, arithmetic and copies ran while one was open for 14% of the time, Pallas kernels for 0%

commit v1 on v0

--- a/solution.py
+++ b/solution.py
@@ -56,7 +56,9 @@
     for part in (w_qkv[:, :half], w_qkv[:, half:]):
         partial_value = jnp.dot(
             normed,
-            lax.all_gather(part, "col", axis=1, tiled=True),
+            jnp.concatenate(
+                lax.all_to_all(jnp.stack([part] * lax.axis_size("col")), "col", 0, 0), axis=1
+            ),
             preferred_element_type=jnp.float32,
         )
         halves.append(row_reduce(partial_value, "row"))

time: 191 us -> 239 us (1.25)
  waiting for transfers between devices: 98 us -> 141 us
  starting transfers between devices: 29.4 us -> 38 us
  local copies, waits for them, and re-layouts: 19.3 us -> 16.6 us
    all_to_all x0 -> x2, waiting for transfers between devices: none -> 80.1 us  [shards(): lax.all_to_all(jnp.stack([part] * lax.axis_size('col')), 'col', 0, 0)]
    all_gather x2 -> x0, waiting for transfers between devices: 56.3 us -> none  [shards(): lax.all_gather(part, 'col', axis=1, tiled=True)]
    all_to_all x2, waiting for transfers between devices: 14.5 us -> 33 us  [row_reduce(): received = lax.all_to_all(pieces, axis_name, 0, 0)]
    all_to_all x0 -> x2, starting transfers between devices: none -> 14.7 us  [shards(): lax.all_to_all(jnp.stack([part] * lax.axis_size('col')), 'col', 0, 0)]
    all_to_all x2, starting transfers between devices: 13.3 us -> 7.31 us  [row_reduce(): received = lax.all_to_all(pieces, axis_name, 0, 0)]
    reshape x4 -> x0, local copies, waits for them, and re-layouts: 4.12 us -> none  [row_reduce(): partial.reshape(rows, count, cols // count).transpose(1, 0, 2).astype(sent)]
    another operation x0 -> x2, local copies, waits for them, and re-layouts: none -> 2.61 us  [shards(): jnp.stack([part] * lax.axis_size('col'))]
  transfers between devices with their start and end apart: 8 -> 8, of which waited for: 6 -> 7; matrix products, arithmetic and copies ran while one was open for 14% -> 8% of each run, Pallas kernels for 0% -> 0%
where the time goes in v1:
time: 239 us; the launch traced here: 238 us
  waiting for transfers between devices  141 us (59%)
  starting transfers between devices  38 us (16%)
  local copies, waits for them, and re-layouts  16.6 us (7%)
  blocking collectives  15.1 us (6%)
  between operations  14.4 us (6%)
  other arithmetic  6.85 us (3%)
  matrix products  6.49 us (3%)
    all_to_all x2, waiting for transfers between devices, shards(): lax.all_to_all(jnp.stack([part] * lax.axis_size('col')), 'col', 0, 0)  80.1 us
    all_to_all x2, waiting for transfers between devices, row_reduce(): received = lax.all_to_all(pieces, axis_name, 0, 0)  33 us
    all_to_all x2, waiting for transfers between devices, row_gather(): return lax.all_to_all(copies, axis_name, 0, 0)  17.4 us
    all_to_all x1, blocking collectives, row_reduce(): received = lax.all_to_all(pieces, axis_name, 0, 0)  15.1 us
    all_to_all x2, starting transfers between devices, shards(): lax.all_to_all(jnp.stack([part] * lax.axis_size('col')), 'col', 0, 0)  14.7 us
    all_to_all x2, starting transfers between devices, row_gather(): return lax.all_to_all(copies, axis_name, 0, 0)  11.8 us
    all_to_all x1, waiting for transfers between devices, shards(): gathered = lax.all_to_all(packed, 'row', 1, 1)  9.29 us
    all_to_all x2, starting transfers between devices, row_reduce(): received = lax.all_to_all(pieces, axis_name, 0, 0)  7.31 us
  transfers between devices with their start and end apart: 8, of which 7 were waited for; matrix products, arithmetic and copies ran while one was open for 8% of the time, Pallas kernels for 0%

profile of v1, /device:TPU:1, one launch (start us, length us, event | category | flops | bytes accessed | tf_op | source)
XLA Modules:
  0.0 238.0 jit_solution(10289085891021872338)
XLA Ops:
  8.0 7.6 %all-to-all-start = ((f32[16,1,64]{2,1,0:T(1,128)}), f32[16,1,64]{2,1,0:T(1,128)S(1)}, u32[]{:S(2)}, u32[]{:S(2)}) async-start(f32[16,1,64]{2,1,0:T(1,128)} %broadcast_in_dim.88), calls=%async_computation | async-start | bytes 16384 | tf_op jit(solution)/shard_map/all_to_all | solution.py:35
  15.6 1.1 fusion.62
  16.8 5.2 %all-to-all-done = f32[16,1,64]{2,1,0:T(1,128)S(1)} async-done(((f32[16,1,64]{2,1,0:T(1,128)}), f32[16,1,64]{2,1,0:T(1,128)S(1)}, u32[]{:S(2)}, u32[]{:S(2)}) %all-to-all-start) | async-done | bytes 4128 | tf_op jit(solution)/shard_map/all_to_all | solution.py:35
  22.0 1.3 stack.5
  23.3 10.6 %all-to-all-start.3 = ((bf16[16,256,192]{1,2,0:T(8,128)(2,1)}), bf16[16,256,192]{1,2,0:T(8,128)(2,1)S(1)}, u32[]{:S(2)}, u32[]{:S(2)}) async-start(bf16[16,256,192]{1,2,0:T(8,128)(2,1)} %stack.5), calls=%async_computation.3 | async-start | bytes 3145728 | tf_op jit(solution)/shard_map/all_to_all | solution.py:60
  34.0 38.4 %all-to-all-done.3 = bf16[16,256,192]{1,2,0:T(8,128)(2,1)S(1)} async-done(((bf16[16,256,192]{1,2,0:T(8,128)(2,1)}), bf16[16,256,192]{1,2,0:T(8,128)(2,1)S(1)}, u32[]{:S(2)}, u32[]{:S(2)}) %all-to-all-start.3) | async-done | bytes 1572896 | tf_op jit(solution)/shard_map/all_to_all | solution.py:60
  72.4 1.3 stack.4
  73.7 4.1 %all-to-all-start.1 = ((bf16[16,256,192]{1,2,0:T(8,128)(2,1)}), bf16[16,256,192]{1,2,0:T(8,128)(2,1)S(1)}, u32[]{:S(2)}, u32[]{:S(2)}) async-start(bf16[16,256,192]{1,2,0:T(8,128)(2,1)} %stack.4), calls=%async_computation.1 | async-start | bytes 3145728 | tf_op jit(solution)/shard_map/all_to_all | solution.py:60
  78.6 1.6 fusion.11
  80.2 41.7 %all-to-all-done.1 = bf16[16,256,192]{1,2,0:T(8,128)(2,1)S(1)} async-done(((bf16[16,256,192]{1,2,0:T(8,128)(2,1)}), bf16[16,256,192]{1,2,0:T(8,128)(2,1)S(1)}, u32[]{:S(2)}, u32[]{:S(2)}) %all-to-all-start.1) | async-done | bytes 1572896 | tf_op jit(solution)/shard_map/all_to_all | solution.py:60
  121.9 3.7 %all-to-all-start.4 = ((f32[16,64,192]{2,1,0:T(8,128)}), f32[16,64,192]{2,1,0:T(8,128)S(1)}, u32[]{:S(2)}, u32[]{:S(2)}) async-start(f32[16,64,192]{2,1,0:T(8,128)} %fusion.11), calls=%async_computation.4 | async-start | bytes 2097152 | tf_op jit(solution)/shard_map/all_to_all | solution.py:28
  125.5 1.6 fusion.8
  127.2 18.2 %all-to-all-done.4 = f32[16,64,192]{2,1,0:T(8,128)S(1)} async-done(((f32[16,64,192]{2,1,0:T(8,128)}), f32[16,64,192]{2,1,0:T(8,128)S(1)}, u32[]{:S(2)}, u32[]{:S(2)}) %all-to-all-start.4) | async-done | bytes 786464 | tf_op jit(solution)/shard_map/all_to_all | solution.py:28
  145.3 3.7 %all-to-all-start.2 = ((f32[16,64,192]{2,1,0:T(8,128)}), f32[16,64,192]{2,1,0:T(8,128)S(1)}, u32[]{:S(2)}, u32[]{:S(2)}) async-start(f32[16,64,192]{2,1,0:T(8,128)} %fusion.8), calls=%async_computation.2 | async-start | bytes 2097152 | tf_op jit(solution)/shard_map/all_to_all | solution.py:28
  150.9 14.9 %all-to-all-done.2 = f32[16,64,192]{2,1,0:T(8,128)S(1)} async-done(((f32[16,64,192]{2,1,0:T(8,128)}), f32[16,64,192]{2,1,0:T(8,128)S(1)}, u32[]{:S(2)}, u32[]{:S(2)}) %all-to-all-start.2) | async-done | bytes 786464 | tf_op jit(solution)/shard_map/all_to_all | solution.py:28
  167.0 4.3 %all-to-all-start.5 = ((bf16[16,64,384]{2,1,0:T(8,128)(2,1)}), bf16[16,64,384]{2,1,0:T(8,128)(2,1)S(1)}, u32[]{:S(2)}, u32[]{:S(2)}) async-start(bf16[16,64,384]{2,1,0:T(8,128)(2,1)} %broadcast_in_dim.89), calls=%async_computation.5 | async-start | bytes 1572864 | tf_op jit(solution)/shard_map/all_to_all | solution.py:35
  172.0 12.3 %all-to-all-done.5 = bf16[16,64,384]{2,1,0:T(8,128)(2,1)S(1)} async-done(((bf16[16,64,384]{2,1,0:T(8,128)(2,1)}), bf16[16,64,384]{2,1,0:T(8,128)(2,1)S(1)}, u32[]{:S(2)}, u32[]{:S(2)}) %all-to-all-start.5) | async-done | bytes 786464 | tf_op jit(solution)/shard_map/all_to_all | solution.py:35
  189.6 1.5 maximum_maximum_fusion
  191.1 4.2 %all-to-all-start.6 = ((f32[1,16,2,65,128]{4,2,3,0,1:T(2,128)}), f32[1,16,2,65,128]{4,2,3,0,1:T(2,128)S(1)}, u32[]{:S(2)}, u32[]{:S(2)}) async-start(f32[1,16,2,65,128]{4,2,3,0,1:T(2,128)} %maximum_maximum_fusion), calls=%async_computation.6 | async-start | bytes 2129920 | tf_op jit(solution)/shard_map/all_to_all | solution.py:110
  195.5 3.3 %copy.99 = bf16[4096,256]{1,0:T(8,128)(2,1)S(1)} copy(bf16[4096,256]{0,1:T(8,128)(2,1)} %bitcast.128) | data formatting | bytes 4194304 | tf_op jit(solution)/shard_map/dot_general | solution.py:148
  198.8 1.1 copy.113
  201.4 9.3 %all-to-all-done.6 = f32[1,16,2,65,128]{4,2,3,0,1:T(2,128)S(1)} async-done(((f32[1,16,2,65,128]{4,2,3,0,1:T(2,128)}), f32[1,16,2,65,128]{4,2,3,0,1:T(2,128)S(1)}, u32[]{:S(2)}, u32[]{:S(2)}) %all-to-all-start.6) | async-done | bytes 1064992 | tf_op jit(solution)/shard_map/all_to_all | solution.py:110
  211.9 2.2 fusion.24
  215.3 15.1 %all_to_all.41 = bf16[16,64,256]{2,1,0:T(8,128)(2,1)S(1)} all-to-all(bf16[16,64,256]{2,1,0:T(8,128)(2,1)S(1)} %fusion.14), channel_id=1, replica_groups=mesh['row'=16,'col'=16] {'row'}, dimensions={0} | all-to-all | bytes 1048576 | tf_op jit(solution)/shard_map/all_to_all | solution.py:28
  (64 shorter events, 15.5 us)
Async XLA Ops:
  8.0 13.9 %all-to-all-start = ((f32[16,1,64]{2,1,0:T(1,128)}), f32[16,1,64]{2,1,0:T(1,128)S(1)}, u32[]{:S(2)}, u32[]{:S(2)}) async-start(f32[16,1,64]{2,1,0:T(1,128)} %broadcast_in_dim.88), calls=%async_computation | async-start | bytes 16384 | tf_op jit(solution)/shard_map/all_to_all | solution.py:35
  23.3 49.1 %all-to-all-start.3 = ((bf16[16,256,192]{1,2,0:T(8,128)(2,1)}), bf16[16,256,192]{1,2,0:T(8,128)(2,1)S(1)}, u32[]{:S(2)}, u32[]{:S(2)}) async-start(bf16[16,256,192]{1,2,0:T(8,128)(2,1)} %stack.5), calls=%async_computation.3 | async-start | bytes 3145728 | tf_op jit(solution)/shard_map/all_to_all | solution.py:60
  34.0 44.6 %copy-start.6 = (bf16[256]{0:T(256)(128)(2,1)S(1)}, bf16[256]{0:T(256)(128)(2,1)}, u32[]{:S(2)}) copy-start(bf16[256]{0:T(256)(128)(2,1)} %param.9) | copy-start | bytes 1540
  34.0 44.6 %copy-start.4 = (bf16[64,256]{1,0:T(8,128)(2,1)S(1)}, bf16[64,256]{1,0:T(8,128)(2,1)}, u32[]{:S(2)}) copy-start(bf16[64,256]{1,0:T(8,128)(2,1)} %param.8) | copy-start | bytes 98308
  73.7 48.2 %all-to-all-start.1 = ((bf16[16,256,192]{1,2,0:T(8,128)(2,1)}), bf16[16,256,192]{1,2,0:T(8,128)(2,1)S(1)}, u32[]{:S(2)}, u32[]{:S(2)}) async-start(bf16[16,256,192]{1,2,0:T(8,128)(2,1)} %stack.4), calls=%async_computation.1 | async-start | bytes 3145728 | tf_op jit(solution)/shard_map/all_to_all | solution.py:60
  77.8 117.7 %all-gather.2.cloned.1.call-start = ((), (), s32[]{:S(2)}) async-start(), calls=%async_computation.8 | async-start | bytes 2228224 | tf_op jit(solution)/shard_map/all_gather | solution.py:150
  121.9 23.5 %all-to-all-start.4 = ((f32[16,64,192]{2,1,0:T(8,128)}), f32[16,64,192]{2,1,0:T(8,128)S(1)}, u32[]{:S(2)}, u32[]{:S(2)}) async-start(f32[16,64,192]{2,1,0:T(8,128)} %fusion.11), calls=%async_computation.4 | async-start | bytes 2097152 | tf_op jit(solution)/shard_map/all_to_all | solution.py:28
  127.2 22.5 %copy-start.1 = (bf16[1,256,1024]{2,1,0:T(8,128)(2,1)S(1)}, bf16[1,256,1024]{2,1,0:T(8,128)(2,1)}, u32[]{:S(2)}) copy-start(bf16[1,256,1024]{2,1,0:T(8,128)(2,1)} %param.12) | copy-start | bytes 1572868
  127.2 23.4 %copy-start.2 = (bf16[1,256,1024]{2,1,0:T(8,128)(2,1)S(1)}, bf16[1,256,1024]{2,1,0:T(8,128)(2,1)}, u32[]{:S(2)}) copy-start(bf16[1,256,1024]{2,1,0:T(8,128)(2,1)} %param.13) | copy-start | bytes 1572868
  127.2 23.5 %copy-start.5 = (s32[1,64]{1,0:T(1,128)S(1)}, s32[1,64]{1,0:T(1,128)}, u32[]{:S(2)}) copy-start(s32[1,64]{1,0:T(1,128)} %param.15) | copy-start | bytes 772
  145.3 20.5 %all-to-all-start.2 = ((f32[16,64,192]{2,1,0:T(8,128)}), f32[16,64,192]{2,1,0:T(8,128)S(1)}, u32[]{:S(2)}, u32[]{:S(2)}) async-start(f32[16,64,192]{2,1,0:T(8,128)} %fusion.8), calls=%async_computation.2 | async-start | bytes 2097152 | tf_op jit(solution)/shard_map/all_to_all | solution.py:28
  167.0 17.3 %all-to-all-start.5 = ((bf16[16,64,384]{2,1,0:T(8,128)(2,1)}), bf16[16,64,384]{2,1,0:T(8,128)(2,1)S(1)}, u32[]{:S(2)}, u32[]{:S(2)}) async-start(bf16[16,64,384]{2,1,0:T(8,128)(2,1)} %broadcast_in_dim.89), calls=%async_computation.5 | async-start | bytes 1572864 | tf_op jit(solution)/shard_map/all_to_all | solution.py:35
  184.2 2.3 copy-start.3
  184.3 0.9 copy-start
  191.1 19.6 %all-to-all-start.6 = ((f32[1,16,2,65,128]{4,2,3,0,1:T(2,128)}), f32[1,16,2,65,128]{4,2,3,0,1:T(2,128)S(1)}, u32[]{:S(2)}, u32[]{:S(2)}) async-start(f32[1,16,2,65,128]{4,2,3,0,1:T(2,128)} %maximum_maximum_fusion), calls=%async_computation.6 | async-start | bytes 2129920 | tf_op jit(solution)/shard_map/all_to_all | solution.py:110
Sparse Core Ops, SparseCore 0:
  80.4 54.4 all-gather.1
